TPU v7x, 128 devices: a whole 4x4x4 slice. The times are simulated.
128 devices in a mesh: inst: 32 (over x, y, core), arch: 4 (over z).
Axes of the slice: x: 4, y: 4, z: 4, core: 2. Of those that a mesh axis runs over, the one named last changes fastest.
Arguments:
- instance_arch: int32 [8192], P(('inst', 'arch')), may hold values from 0 to 39
- instance_param: int32 [8192], P(('inst', 'arch')), may hold values from 0 to 1023
- instance_ports: int32 [8192, 4], P(('inst', 'arch')), may hold values from 0 to 16383, as said below
- port_row: int32 [16384], replicated, may hold values from 0 to 16383, as said below
- param_table: float32 [1024, 64], replicated, may hold values from 0.5 to 2
- bubble_inverse: float32 [40, 64, 64], P('arch'), as said below
- coupling: float32 [40, 64, 128], P('arch'), may hold values from -0.75 to 0.75
- port_stiffness: float32 [40, 128, 128], P('arch'), as said below
- coupling_offset: float32 [8192, 64, 128], P(('inst', 'arch')), may hold values from -0.375 to 0.375
Outputs:
- assembled: float32 [16384, 7168], P(('inst', 'arch'))
Inputs may be any that keep to these rules, and one draw needn't show every extreme that they name: `instance_ports`: every port is named exactly twice: once at slot 0 and once at slot 1 of two different instances, or once at slot 2 and once at slot 3 of two different instances; an instance's four ports are distinct. `port_row`: A permutation of the ports. Among the 256 port slots of one device's instances, at most 3 name ports whose row lies in one device's (128) rows, and this many is reached. `bubble_inverse`: each matrix is symmetric. `port_stiffness`: each matrix is symmetric.
All inputs are finite; a program needn't handle non-finite values.
Results may differ from a plain program's by a relative error of at most 0.00013.
Values sent between devices are 32-bit elements; how exact they have to be, the bound alone decides.
A program may use at most 128 MiB of HBM per device.

v0:
```python
import jax
import jax.numpy as jnp
import numpy as np
from jax import lax
from jax.sharding import PartitionSpec as P


def orders(width):
    result = []
    for which in range(4):
        parts = [np.arange(which * width, (which + 1) * width)]
        for other in range(4):
            if other != which:
                parts.append(np.arange(other * width, (other + 1) * width))
        result.append(np.concatenate(parts))
    return result


def condense(inverses, couplings, stiffness, table, arch_ids, param_ids, offsets):
    scales = jnp.take(table, param_ids, axis=0)
    weighted = scales[:, :, None] * (jnp.take(couplings, arch_ids, axis=0) + offsets)
    applied = jnp.einsum(
        "bmn,bnq->bmq",
        jnp.take(inverses, arch_ids, axis=0),
        weighted,
        precision=lax.Precision.HIGHEST,
    )
    return jnp.take(stiffness, arch_ids, axis=0) - jnp.einsum(
        "bmp,bmq->bpq", weighted, applied, precision=lax.Precision.HIGHEST
    )


def body(
    instance_arch,
    instance_param,
    instance_ports,
    port_row,
    param_table,
    bubble_inverse,
    coupling,
    port_stiffness,
    coupling_offset,
):
    instances = instance_arch.shape[0]
    width = port_stiffness.shape[1] // 4
    flat_width = 4 * width * width
    inverses, couplings, stiffness = (
        lax.all_gather(bubble_inverse, "arch", axis=0, tiled=True),
        lax.all_gather(coupling, "arch", axis=0, tiled=True),
        lax.all_gather(port_stiffness, "arch", axis=0, tiled=True),
    )
    schur = condense(
        inverses, couplings, stiffness, param_table, instance_arch, instance_param, coupling_offset
    )
    columns = orders(width)
    strips = jnp.concatenate(
        [
            schur[:, which * width : (which + 1) * width, :][:, :, columns[which]]
            for which in range(4)
        ],
        axis=0,
    )
    strips = strips.reshape(4 * instances, flat_width)
    row_ids = jnp.take(port_row, instance_ports, axis=0).T.reshape(4 * instances)
    slot_ids = jnp.repeat(jnp.arange(4, dtype=jnp.int32), instances)
    row_codes = row_ids * 4 + slot_ids
    inst_count = lax.axis_size("inst")
    arch_count = lax.axis_size("arch")
    owners = inst_count * arch_count
    port_count = 2 * instances
    capacity = 4 * instances // owners * 3 // 2
    owner_ids = row_ids // port_count
    owner_hits = (owner_ids[:, None] == jnp.arange(owners, dtype=jnp.int32)[None, :]).astype(
        jnp.int32
    )
    ordinal = jnp.sum((jnp.cumsum(owner_hits, axis=0) - 1) * owner_hits, axis=1)
    buffer_slot = owner_ids * capacity + ordinal
    chosen = buffer_slot[None, :] == jnp.arange(owners * capacity, dtype=jnp.int32)[:, None]
    outgoing = jnp.dot(
        chosen.astype(jnp.float32),
        strips,
        precision=lax.Precision.HIGHEST,
        preferred_element_type=jnp.float32,
    )
    filled = jnp.any(chosen, axis=1)
    out_codes = jnp.where(filled, jnp.sum(jnp.where(chosen, row_codes[None, :], 0), axis=1), -1)
    incoming, in_codes = (
        lax.all_to_all(
            outgoing.reshape(owners, capacity, flat_width),
            ("inst", "arch"),
            split_axis=0,
            concat_axis=0,
            tiled=True,
        ),
        lax.all_to_all(
            out_codes.reshape(owners, capacity),
            ("inst", "arch"),
            split_axis=0,
            concat_axis=0,
            tiled=True,
        ),
    )
    incoming = incoming.reshape(owners * capacity, flat_width)
    in_codes = in_codes.reshape(owners * capacity)
    my_index = lax.axis_index("inst") * arch_count + lax.axis_index("arch")
    live_slot = in_codes >= 0
    local_row = jnp.where(live_slot, in_codes // 4 - my_index * port_count, port_count)
    parity = in_codes % 4 % 2
    even_index = jnp.where(live_slot & (parity == 0), local_row, port_count)
    odd_index = jnp.where(live_slot & (parity == 1), local_row, port_count)
    targets = jnp.arange(port_count, dtype=jnp.int32)[:, None]
    placing = jnp.concatenate(
        [
            local_row[None, :] == targets,
            even_index[None, :] == targets,
            odd_index[None, :] == targets,
        ],
        axis=0,
    )
    placed = jnp.dot(
        placing.astype(jnp.float32),
        incoming,
        precision=lax.Precision.HIGHEST,
        preferred_element_type=jnp.float32,
    )
    placed = placed.reshape(3, port_count, width, 4 * width)
    joined = jnp.concatenate(
        [placed[0, :, :, :width], placed[1, :, :, width:], placed[2, :, :, width:]], axis=2
    )
    return joined.reshape(port_count, 7 * width * width)


def solution(mesh):
    return jax.shard_map(
        body,
        mesh=mesh,
        in_specs=(
            P(("inst", "arch")),
            P(("inst", "arch")),
            P(("inst", "arch"), None),
            P(),
            P(),
            P("arch", None, None),
            P("arch", None, None),
            P("arch", None, None),
            P(("inst", "arch"), None, None),
        ),
        out_specs=P(("inst", "arch"), None),
        check_vma=False,
    )
```

profile of v0, /device:TPU:6, one launch (start us, length us, event | category | flops | bytes accessed | tf_op | source)
XLA Modules:
  0.0 307.8 jit_solution(5884704730045930546)
XLA Ops:
  6.5 0.7 all-gather.5.cloned.1.call-update
  7.3 0.7 all-gather.3.cloned.1.call-update
  8.0 0.7 compare_select_fusion
  8.7 0.1 copy.92
  8.8 0.1 reshape.302
  9.0 1.7 gather_fusion
  10.7 0.1 reshape.301
  11.0 0.1 copy.94
  11.1 0.2 fusion.9
  11.7 0.2 fusion.10
  11.8 0.2 fusion.4
  12.0 0.1 select_reduce_fusion
  12.2 0.8 select_n.162
  13.0 10.5 %all-to-all-start = ((s32[128,1,3]{2,1,0:T(1,128)}), s32[128,1,3]{2,1,0:T(1,128)S(1)}, u32[]{:S(2)}, u32[]{:S(2)}) async-start(s32[128,1,3]{2,1,0:T(1,128)} %bitcast.4), calls=%async_computation | async-start | bytes 131072 | tf_op jit(solution)/shard_map/all_to_all | solution.py:95
  23.5 0.2 copy.97
  23.7 0.6 gather_fusion.2
  24.4 22.8 %all_gather.11 = f32[40,64,64]{2,1,0:T(8,128)S(1)} all-gather(f32[10,64,64]{2,1,0:T(8,128)S(1)} %copy-done.3), channel_id=1, replica_groups=mesh['inst'=32,'arch'=4] {'arch'}, dimensions={0}, use_global_device_ids=true | all-gather | bytes 819200 | tf_op jit(solution)/shard_map/all_gather | solution.py:48
  47.2 2.0 gather_fusion.4
  49.4 2.0 gather_fusion.3
  51.4 6.2 %fusion = f32[64,64,128]{2,1,0:T(8,128)} fusion(f32[64,64,64]{2,1,0:T(8,128)} %gather_fusion.4, pred[64]{0:T(512)(128)(4,1)S(1)} %compare_and_fusion.1, f32[64,64,128]{2,1,0:T(8,128)} %param.25, f32[64,64,128]{2,1,0:T(8,128)S(1)} %gather_fusion.3, f32[64,64]{1,0:T(8,128)S(1)} %broadcast_select_fusion), kind=kOutput, calls=%fused_computation.12 | convolution fusion | flops 404488192 | bytes 7356480 | tf_op jit(solution)/shard_map/bmn,bnq->bmq/dot_general | solution.py:22
  57.6 22.4 %all-gather.3.cloned.1.call-done = f32[40,128,128]{2,1,0:T(8,128)} async-done(((f32[10,128,128]{2,1,0:T(8,128)}), f32[40,128,128]{2,1,0:T(8,128)}) %all-gather.3.cloned.1.call-update) | async-done | bytes 2621456 | tf_op jit(solution)/shard_map/all_gather | solution.py:50
  79.9 4.6 %gather_fusion.1 = f32[64,128,128]{2,1,0:T(8,128)} fusion(f32[40,128,128]{2,1,0:T(8,128)} %all-gather.3.cloned.1.call-done, s32[1024]{0:T(1024)S(1)} %pad_clamp_fusion.5), kind=kCustom, calls=%fused_computation.1 | custom fusion | bytes 8388864 | tf_op jit(solution)/shard_map/jit(_take)/gather | solution.py:28
  84.6 11.6 %select_subtract_fusion = f32[64,128,128]{2,1,0:T(8,128)S(1)} fusion(f32[64,128,128]{2,1,0:T(8,128)} %gather_fusion.1, f32[64,64,128]{2,1,0:T(8,128)} %fusion, pred[64]{0:T(512)(128)(4,1)S(1)} %compare_and_fusion.1, f32[64,64,128]{2,1,0:T(8,128)} %param.25, f32[64,64,128]{2,1,0:T(8,128)S(1)} %gather_fusion.3, f32[64,64]{1,0:T(8,128)S(1)} %broadcast_select_fusion), kind=kOutput, calls=%fused_computation.10 | convolution fusion | flops 808976384 | bytes 14696512 | tf_op jit(solution)/shard_map/bmp,bmq->bpq/dot_general | solution.py:28
  96.1 1.4 fusion.20
  97.6 3.1 %copy.98 = f32[64,32,128]{0,1,2:T(8,128)} copy(f32[64,32,128]{2,1,0:T(8,128)S(1)} %get-tuple-element.9) | data formatting | bytes 2097152 | tf_op jit(solution)/shard_map/slice | solution.py:58
  100.7 2.9 copy.101
  103.6 3.0 copy.100
  106.7 2.9 copy.99
  109.6 3.6 %gather_fusion.5 = f32[128,64,32]{1,2,0:T(8,128)} fusion(f32[64,32,128]{0,1,2:T(8,128)} %copy.98, s32[1024]{0:T(1024)S(1)} %pad_clamp_fusion.3), kind=kCustom, calls=%fused_computation.5 | custom fusion | bytes 2097664 | tf_op jit(solution)/shard_map/gather | solution.py:58
  113.2 3.6 %gather_fusion.8 = f32[128,64,32]{1,2,0:T(8,128)} fusion(f32[64,32,128]{0,1,2:T(8,128)} %copy.101, s32[1024]{0:T(1024)S(1)} %pad_clamp_fusion), kind=kCustom, calls=%fused_computation.8 | custom fusion | bytes 2097664 | tf_op jit(solution)/shard_map/gather | solution.py:58
  116.8 2.1 gather_fusion.7
  118.9 3.7 %gather_fusion.6 = f32[128,64,32]{1,2,0:T(8,128)} fusion(f32[64,32,128]{0,1,2:T(8,128)} %copy.99, s32[1024]{0:T(1024)S(1)} %pad_clamp_fusion.2), kind=kCustom, calls=%fused_computation.6 | custom fusion | bytes 2097664 | tf_op jit(solution)/shard_map/gather | solution.py:58
  122.6 6.6 %pad_maximum_fusion = f32[256,32,128]{0,1,2:T(8,128)} fusion(f32[64,32,128]{0,1,2:T(8,128)} %bitcast.39, f32[64,32,128]{0,1,2:T(8,128)} %bitcast.40, f32[64,32,128]{0,1,2:T(8,128)} %bitcast.41, f32[64,32,128]{0,1,2:T(8,128)S(1)} %bitcast.38), kind=kLoop, calls=%fused_computation.9 | loop fusion | flops 3145728 | bytes 8388608 | tf_op jit(solution)/shard_map/concatenate | solution.py:56
  129.2 5.9 %copy.102 = f32[256,32,128]{2,1,0:T(8,128)} copy(f32[256,32,128]{0,1,2:T(8,128)} %pad_maximum_fusion) | data formatting | bytes 8388608 | tf_op jit(solution)/shard_map/concatenate | solution.py:56
  135.1 5.0 %reshape.378 = f32[256,4096,1]{1,0,2:T(8,128)} reshape(f32[256,32,128]{2,1,0:T(8,128)} %copy.102) | data formatting | bytes 8388608 | tf_op jit(solution)/shard_map/reshape | solution.py:63
  140.1 4.8 %fusion.5 = f32[128,3,4096]{2,0,1:T(8,128)S(1)} fusion(f32[256,4096,1]{1,0,2:T(8,128)} %reshape.378, s32[128,3]{0,1:T(4,128)S(1)} %multiply_add_fusion, s32[256]{0:T(256)S(1)} %multiply_add_fusion.2), kind=kOutput, calls=%fused_computation.24 | convolution fusion | flops 4831936512 | bytes 10488320 | tf_op jit(solution)/shard_map/dot_general | solution.py:79
  144.9 7.5 %copy.103 = f32[128,3,4096]{2,1,0:T(4,128)} copy(f32[128,3,4096]{2,0,1:T(8,128)S(1)} %fusion.5) | data formatting | bytes 12582912 | tf_op jit(solution)/shard_map/dot_general | solution.py:79
  152.5 8.6 %all-to-all-start.1 = ((f32[128,3,4096]{2,1,0:T(4,128)}), f32[128,3,4096]{2,1,0:T(4,128)}, u32[]{:S(2)}, u32[]{:S(2)}) async-start(f32[128,3,4096]{2,1,0:T(4,128)} %copy.103), calls=%async_computation.1 | async-start | bytes 16777216 | tf_op jit(solution)/shard_map/all_to_all | solution.py:88
  161.1 0.5 broadcast.419
  161.6 0.8 reduce.3
  162.4 0.2 reshape.296
  162.8 106.3 %all-to-all-done.1 = f32[128,3,4096]{2,1,0:T(4,128)} async-done(((f32[128,3,4096]{2,1,0:T(4,128)}), f32[128,3,4096]{2,1,0:T(4,128)}, u32[]{:S(2)}, u32[]{:S(2)}) %all-to-all-start.1) | async-done | bytes 6291488 | tf_op jit(solution)/shard_map/all_to_all | solution.py:88
  269.1 9.5 %reshape.298 = f32[384,4096]{1,0:T(8,128)} reshape(f32[128,3,4096]{2,1,0:T(4,128)} %all-to-all-done.1) | data formatting | bytes 12582912 | tf_op jit(solution)/shard_map/reshape | solution.py:103
  278.6 6.6 %copy.104 = f32[4096,384]{1,0:T(8,128)} copy(f32[4096,384]{0,1:T(8,128)} %bitcast.36) | data formatting | bytes 12582912 | tf_op jit(solution)/shard_map/dot_general | solution.py:120
  285.2 8.1 %fusion.21 = f32[3,128,32,128]{1,3,2,0:T(8,128)S(1)} fusion(pred[3,128,384,1]{2,1,3,0:T(32,128)(4,1)S(1)} %bitcast.42, f32[32,128,384,1]{2,1,0,3:T(8,128)} %bitcast.35), kind=kOutput, calls=%fused_computation.86 | convolution fusion | flops 7247757312 | bytes 12730368 | tf_op jit(solution)/shard_map/dot_general | solution.py:120
  293.4 0.3 slice_bitcast_fusion.1
  293.7 2.0 pad_maximum_fusion.1
  295.7 5.3 %copy.105 = f32[128,7168]{1,0:T(8,128)} copy(f32[128,7168]{0,1:T(8,128)} %bitcast.37) | data formatting | bytes 7340032 | tf_op jit(solution)/shard_map/reshape | solution.py:130
  (61 shorter events, 0.9 us)
Async XLA Ops:
  6.5 2.4 copy-start
  6.5 42.8 %all-gather.5.cloned.1.call-start = ((), (), s32[]{:S(2)}) async-start(), calls=%async_computation.3 | async-start | bytes 1638400 | tf_op jit(solution)/shard_map/all_gather | solution.py:49
  7.3 72.7 %all-gather.3.cloned.1.call-start = ((), (), s32[]{:S(2)}) async-start(), calls=%async_computation.2 | async-start | bytes 3276800 | tf_op jit(solution)/shard_map/all_gather | solution.py:50
  8.9 2.0 copy-start.5
  8.9 14.6 %copy-start.4 = (f32[1024,64]{0,1:T(8,128)S(1)}, f32[1024,64]{0,1:T(8,128)}, u32[]{:S(2)}) copy-start(f32[1024,64]{0,1:T(8,128)} %param.21) | copy-start | bytes 786436
  8.9 14.8 %copy-start.10 = (s32[64]{0:T(128)S(1)}, s32[64]{0:T(128)}, u32[]{:S(2)}) copy-start(s32[64]{0:T(128)} %param.18) | copy-start | bytes 772
  10.7 13.6 %copy-start.9 = (s32[64]{0:T(128)S(1)}, s32[64]{0:T(128)}, u32[]{:S(2)}) copy-start(s32[64]{0:T(128)} %param.17) | copy-start | bytes 772
  10.7 13.7 %copy-start.3 = (f32[10,64,64]{2,1,0:T(8,128)S(1)}, f32[10,64,64]{2,1,0:T(8,128)}, u32[]{:S(2)}) copy-start(f32[10,64,64]{2,1,0:T(8,128)} %param.22) | copy-start | bytes 491524
  13.0 139.4 %all-to-all-start = ((s32[128,1,3]{2,1,0:T(1,128)}), s32[128,1,3]{2,1,0:T(1,128)S(1)}, u32[]{:S(2)}, u32[]{:S(2)}) async-start(s32[128,1,3]{2,1,0:T(1,128)} %bitcast.4), calls=%async_computation | async-start | bytes 131072 | tf_op jit(solution)/shard_map/all_to_all | solution.py:95
  47.2 2.0 copy-start.8
  47.2 2.0 copy-start.7
  47.2 2.1 copy-start.6
  118.9 3.7 %copy-start.2 = (f32[128,64,32]{1,2,0:T(8,128)S(1)}, f32[128,64,32]{1,2,0:T(8,128)}, u32[]{:S(2)}) copy-start(f32[128,64,32]{1,2,0:T(8,128)} %gather_fusion.5) | copy-start | bytes 3145732
  152.5 116.6 %all-to-all-start.1 = ((f32[128,3,4096]{2,1,0:T(4,128)}), f32[128,3,4096]{2,1,0:T(4,128)}, u32[]{:S(2)}, u32[]{:S(2)}) async-start(f32[128,3,4096]{2,1,0:T(4,128)} %copy.103), calls=%async_computation.1 | async-start | bytes 16777216 | tf_op jit(solution)/shard_map/all_to_all | solution.py:88
  295.7 5.3 %copy-start.1 = (s32[16384]{0:T(1024)S(1)}, s32[16384]{0:T(1024)}, u32[]{:S(2)}) copy-start(s32[16384]{0:T(1024)} %param.20) | copy-start | bytes 196612
Sparse Core Ops, SparseCore 0:
  9.0 33.6 all-gather.4
  44.4 35.4 all-gather.2
where the time goes:
time: 309 us; the launch traced here: 308 us
  waiting for transfers between devices  130 us (42%)
  local copies, waits for them, and re-layouts  80.1 us (26%)
  matrix products  30.7 us (10%)
  blocking collectives  22.8 us (7%)
  starting transfers between devices  19.1 us (6%)
  between operations  13.8 us (4%)
  other arithmetic  11.2 us (4%)
    all_to_all x1, waiting for transfers between devices, body(): lax.all_to_all(outgoing.reshape(owners, capacity, flat_width), ('inst', '...  106 us
    all_gather x1, blocking collectives, body(): lax.all_gather(bubble_inverse, 'arch', axis=0, tiled=True)  22.8 us
    all_gather x1, waiting for transfers between devices, body(): lax.all_gather(port_stiffness, 'arch', axis=0, tiled=True)  22.4 us
    slice x5, local copies, waits for them, and re-layouts, body(): schur[:, which * width:(which + 1) * width, :][:, :, columns[which]]  13.4 us
    gather x4, local copies, waits for them, and re-layouts, body(): schur[:, which * width:(which + 1) * width, :][:, :, columns[which]]  13 us
    dot_general x1, matrix products, condense(): jnp.einsum('bmp,bmq->bpq', weighted, applied, precision=lax.Precision.HIG...  11.6 us
    all_to_all x1, starting transfers between devices, body(): lax.all_to_all(out_codes.reshape(owners, capacity), ('inst', 'arch'), spl...  10.5 us
    reshape x1, local copies, waits for them, and re-layouts, body(): incoming = incoming.reshape(owners * capacity, flat_width)  9.5 us
  transfers between devices with their start and end apart: 4, of which 2 were waited for; matrix products, arithmetic and copies ran while one was open for 29% of the time, Pallas kernels for 0%

commit v1 on v0

--- a/solution.py
+++ b/solution.py
@@ -47,7 +47,10 @@
     inverses, couplings, stiffness = (
         lax.all_gather(bubble_inverse, "arch", axis=0, tiled=True),
         lax.all_gather(coupling, "arch", axis=0, tiled=True),
-        lax.all_gather(port_stiffness, "arch", axis=0, tiled=True),
+        jnp.concatenate(
+            lax.all_to_all(jnp.stack([port_stiffness] * lax.axis_size("arch")), "arch", 0, 0),
+            axis=0,
+        ),
     )
     schur = condense(
         inverses, couplings, stiffness, param_table, instance_arch, instance_param, coupling_offset

time: 309 us -> 316 us (1.023)
  blocking collectives: 22.8 us -> 49.3 us
  waiting for transfers between devices: 130 us -> 106 us
  starting transfers between devices: 19.1 us -> 23.8 us
  matrix products: 30.7 us -> 26.4 us
  local copies, waits for them, and re-layouts: 80.1 us -> 83.5 us
    all_gather x1, blocking collectives: 22.8 us -> 49.3 us  [body(): lax.all_gather(bubble_inverse, 'arch', axis=0, tiled=True)]
    all_gather x1 -> x0, waiting for transfers between devices: 22.4 us -> none  [body(): lax.all_gather(port_stiffness, 'arch', axis=0, tiled=True)]
    all_to_all x0 -> x1, starting transfers between devices: none -> 5.44 us  [body(): lax.all_to_all(jnp.stack([port_stiffness] * lax.axis_size('arch')), 'arch...]
    dot_general x1, matrix products: 11.6 us -> 8.33 us  [condense(): jnp.einsum('bmp,bmq->bpq', weighted, applied, precision=lax.Precision.HIG...]
  transfers between devices with their start and end apart: 4 -> 4, of which waited for: 2 -> 1; matrix products, arithmetic and copies ran while one was open for 29% -> 28% of each run, Pallas kernels for 0% -> 0%
where the time goes in v1:
time: 316 us; the launch traced here: 314 us
  waiting for transfers between devices  106 us (34%)
  local copies, waits for them, and re-layouts  83.5 us (26%)
  blocking collectives  49.3 us (16%)
  matrix products  26.4 us (8%)
  starting transfers between devices  23.8 us (8%)
  between operations  13.8 us (4%)
  other arithmetic  10.5 us (3%)
    all_to_all x1, waiting for transfers between devices, body(): lax.all_to_all(outgoing.reshape(owners, capacity, flat_width), ('inst', '...  106 us
    all_gather x1, blocking collectives, body(): lax.all_gather(bubble_inverse, 'arch', axis=0, tiled=True)  49.3 us
    slice x5, local copies, waits for them, and re-layouts, body(): schur[:, which * width:(which + 1) * width, :][:, :, columns[which]]  13.4 us
    gather x4, local copies, waits for them, and re-layouts, body(): schur[:, which * width:(which + 1) * width, :][:, :, columns[which]]  13 us
    all_to_all x1, starting transfers between devices, body(): lax.all_to_all(outgoing.reshape(owners, capacity, flat_width), ('inst', '...  10.2 us
    reshape x1, local copies, waits for them, and re-layouts, body(): incoming = incoming.reshape(owners * capacity, flat_width)  9.5 us
    dot_general x1, matrix products, condense(): jnp.einsum('bmp,bmq->bpq', weighted, applied, precision=lax.Precision.HIG...  8.33 us
    dot_general x1, matrix products, body(): jnp.dot(placing.astype(jnp.float32), incoming, precision=lax.Precision.HI...  8.14 us
  transfers between devices with their start and end apart: 4, of which 1 were waited for; matrix products, arithmetic and copies ran while one was open for 28% of the time, Pallas kernels for 0%

profile of v1, /device:TPU:6, one launch (start us, length us, event | category | flops | bytes accessed | tf_op | source)
XLA Modules:
  0.0 313.7 jit_solution(11881706867353487767)
XLA Ops:
  6.5 0.7 all-gather.2.cloned.1.call-update
  7.3 2.9 stack.2
  10.1 5.4 %all-to-all-start.1 = ((f32[4,10,128,128]{3,2,1,0:T(8,128)}), f32[4,10,128,128]{3,2,1,0:T(8,128)S(1)}, u32[]{:S(2)}, u32[]{:S(2)}) async-start(f32[4,10,128,128]{3,2,1,0:T(8,128)} %stack.2), calls=%async_computation.1 | async-start | bytes 5242880 | tf_op jit(solution)/shard_map/all_to_all | solution.py:51
  15.6 0.1 copy.92
  15.7 0.1 reshape.308
  15.8 1.7 gather_fusion
  17.6 0.1 reshape.307
  17.8 0.1 reshape.298
  18.0 0.1 copy.94
  18.2 0.2 fusion.9
  18.5 0.2 fusion.10
  18.7 0.2 fusion.4
  18.9 0.1 select_reduce_fusion
  19.1 0.8 select_n.162
  19.9 1.2 copy.97
  21.1 0.6 gather_fusion.2
  21.7 49.3 %all_gather.7 = f32[40,64,64]{2,1,0:T(8,128)} all-gather(f32[10,64,64]{2,1,0:T(8,128)S(1)} %copy-done.5), channel_id=1, replica_groups=mesh['inst'=32,'arch'=4] {'arch'}, dimensions={0}, use_global_device_ids=true | all-gather | bytes 819200 | tf_op jit(solution)/shard_map/all_gather | solution.py:48
  71.1 3.3 %gather_fusion.4 = f32[64,64,64]{2,1,0:T(8,128)} fusion(f32[40,64,64]{2,1,0:T(8,128)} %all_gather.7, s32[1024]{0:T(1024)S(1)} %pad_clamp_fusion.5), kind=kCustom, calls=%fused_computation.4 | custom fusion | bytes 2097408 | tf_op jit(solution)/shard_map/jit(_take)/gather | solution.py:24
  74.6 8.1 %all-to-all-start = ((s32[128,1,3]{2,1,0:T(1,128)}), s32[128,1,3]{2,1,0:T(1,128)S(1)}, u32[]{:S(2)}, u32[]{:S(2)}) async-start(s32[128,1,3]{2,1,0:T(1,128)} %bitcast.4), calls=%async_computation | async-start | bytes 131072 | tf_op jit(solution)/shard_map/all_to_all | solution.py:98
  82.7 2.8 gather_fusion.1
  85.5 2.0 gather_fusion.3
  87.6 4.9 %fusion = f32[64,64,128]{2,1,0:T(8,128)S(1)} fusion(f32[64,64,64]{2,1,0:T(8,128)} %gather_fusion.4, pred[64]{0:T(512)(128)(4,1)S(1)} %compare_and_fusion.1, f32[64,64,128]{2,1,0:T(8,128)} %param.25, f32[64,64,128]{2,1,0:T(8,128)S(1)} %gather_fusion.3, f32[64,64]{1,0:T(8,128)S(1)} %broadcast_select_fusion), kind=kOutput, calls=%fused_computation.12 | convolution fusion | flops 404488192 | bytes 7356480 | tf_op jit(solution)/shard_map/bmn,bnq->bmq/dot_general | solution.py:22
  92.5 8.3 %select_subtract_fusion = f32[64,128,128]{2,1,0:T(8,128)S(1)} fusion(f32[64,128,128]{2,1,0:T(8,128)S(1)} %copy-done.2, f32[64,64,128]{2,1,0:T(8,128)S(1)} %fusion, pred[64]{0:T(512)(128)(4,1)S(1)} %compare_and_fusion.1, f32[64,64,128]{2,1,0:T(8,128)S(1)} %copy-done.3, f32[64,64,128]{2,1,0:T(8,128)S(1)} %gather_fusion.3, f32[64,64]{1,0:T(8,128)S(1)} %broadcast_select_fusion), kind=kOutput, calls=%fused_computation.10 | convolution fusion | flops 808976384 | bytes 14696512 | tf_op jit(solution)/shard_map/bmp,bmq->bpq/dot_general | solution.py:28
  100.8 1.4 fusion.20
  102.3 3.1 %copy.98 = f32[64,32,128]{0,1,2:T(8,128)} copy(f32[64,32,128]{2,1,0:T(8,128)S(1)} %get-tuple-element.9) | data formatting | bytes 2097152 | tf_op jit(solution)/shard_map/slice | solution.py:61
  105.4 2.9 copy.101
  108.3 3.0 copy.100
  111.4 2.9 copy.99
  114.3 3.6 %gather_fusion.5 = f32[128,64,32]{1,2,0:T(8,128)} fusion(f32[64,32,128]{0,1,2:T(8,128)} %copy.98, s32[1024]{0:T(1024)S(1)} %pad_clamp_fusion.3), kind=kCustom, calls=%fused_computation.5 | custom fusion | bytes 2097664 | tf_op jit(solution)/shard_map/gather | solution.py:61
  117.9 3.6 %gather_fusion.8 = f32[128,64,32]{1,2,0:T(8,128)} fusion(f32[64,32,128]{0,1,2:T(8,128)} %copy.101, s32[1024]{0:T(1024)S(1)} %pad_clamp_fusion), kind=kCustom, calls=%fused_computation.8 | custom fusion | bytes 2097664 | tf_op jit(solution)/shard_map/gather | solution.py:61
  121.5 2.1 gather_fusion.7
  123.6 3.7 %gather_fusion.6 = f32[128,64,32]{1,2,0:T(8,128)} fusion(f32[64,32,128]{0,1,2:T(8,128)} %copy.99, s32[1024]{0:T(1024)S(1)} %pad_clamp_fusion.2), kind=kCustom, calls=%fused_computation.6 | custom fusion | bytes 2097664 | tf_op jit(solution)/shard_map/gather | solution.py:61
  127.3 6.6 %pad_maximum_fusion = f32[256,32,128]{0,1,2:T(8,128)} fusion(f32[64,32,128]{0,1,2:T(8,128)} %bitcast.41, f32[64,32,128]{0,1,2:T(8,128)} %bitcast.42, f32[64,32,128]{0,1,2:T(8,128)} %bitcast.43, f32[64,32,128]{0,1,2:T(8,128)S(1)} %bitcast.40), kind=kLoop, calls=%fused_computation.9 | loop fusion | flops 3145728 | bytes 8388608 | tf_op jit(solution)/shard_map/concatenate | solution.py:59
  133.9 5.9 %copy.102 = f32[256,32,128]{2,1,0:T(8,128)} copy(f32[256,32,128]{0,1,2:T(8,128)} %pad_maximum_fusion) | data formatting | bytes 8388608 | tf_op jit(solution)/shard_map/concatenate | solution.py:59
  139.9 5.0 %reshape.384 = f32[256,4096,1]{1,0,2:T(8,128)} reshape(f32[256,32,128]{2,1,0:T(8,128)} %copy.102) | data formatting | bytes 8388608 | tf_op jit(solution)/shard_map/reshape | solution.py:66
  144.8 5.0 %fusion.5 = f32[128,3,4096]{2,0,1:T(8,128)S(1)} fusion(f32[256,4096,1]{1,0,2:T(8,128)} %reshape.384, s32[128,3]{0,1:T(4,128)S(1)} %multiply_add_fusion, s32[256]{0:T(256)S(1)} %multiply_add_fusion.2), kind=kOutput, calls=%fused_computation.24 | convolution fusion | flops 4831936512 | bytes 10488320 | tf_op jit(solution)/shard_map/dot_general | solution.py:82
  149.9 7.5 %copy.103 = f32[128,3,4096]{2,1,0:T(4,128)} copy(f32[128,3,4096]{2,0,1:T(8,128)S(1)} %fusion.5) | data formatting | bytes 12582912 | tf_op jit(solution)/shard_map/dot_general | solution.py:82
  157.4 10.2 %all-to-all-start.2 = ((f32[128,3,4096]{2,1,0:T(4,128)}), f32[128,3,4096]{2,1,0:T(4,128)}, u32[]{:S(2)}, u32[]{:S(2)}) async-start(f32[128,3,4096]{2,1,0:T(4,128)} %copy.103), calls=%async_computation.2 | async-start | bytes 16777216 | tf_op jit(solution)/shard_map/all_to_all | solution.py:91
  167.7 0.5 broadcast.421
  168.2 0.8 reduce.3
  169.0 0.2 reshape.301
  169.4 105.6 %all-to-all-done.2 = f32[128,3,4096]{2,1,0:T(4,128)} async-done(((f32[128,3,4096]{2,1,0:T(4,128)}), f32[128,3,4096]{2,1,0:T(4,128)}, u32[]{:S(2)}, u32[]{:S(2)}) %all-to-all-start.2) | async-done | bytes 6291488 | tf_op jit(solution)/shard_map/all_to_all | solution.py:91
  275.0 9.5 %reshape.304 = f32[384,4096]{1,0:T(8,128)} reshape(f32[128,3,4096]{2,1,0:T(4,128)} %all-to-all-done.2) | data formatting | bytes 12582912 | tf_op jit(solution)/shard_map/reshape | solution.py:106
  284.5 6.6 %copy.104 = f32[4096,384]{1,0:T(8,128)} copy(f32[4096,384]{0,1:T(8,128)} %bitcast.37) | data formatting | bytes 12582912 | tf_op jit(solution)/shard_map/dot_general | solution.py:123
  291.1 8.1 %fusion.21 = f32[3,128,32,128]{1,3,2,0:T(8,128)S(1)} fusion(pred[3,128,384,1]{2,1,3,0:T(32,128)(4,1)S(1)} %bitcast.44, f32[32,128,384,1]{2,1,0,3:T(8,128)} %bitcast.36), kind=kOutput, calls=%fused_computation.86 | convolution fusion | flops 7247757312 | bytes 12730368 | tf_op jit(solution)/shard_map/dot_general | solution.py:123
  299.3 0.3 slice_bitcast_fusion.1
  299.6 2.0 pad_maximum_fusion.1
  301.6 5.3 %copy.105 = f32[128,7168]{1,0:T(8,128)} copy(f32[128,7168]{0,1:T(8,128)} %bitcast.39) | data formatting | bytes 7340032 | tf_op jit(solution)/shard_map/reshape | solution.py:133
  (63 shorter events, 0.8 us)
Async XLA Ops:
  6.5 9.3 %copy-start = (s32[16384]{0:T(1024)S(1)}, s32[16384]{0:T(1024)}, u32[]{:S(2)}) copy-start(s32[16384]{0:T(1024)} %param.20) | copy-start | bytes 196612
  6.5 79.0 %all-gather.2.cloned.1.call-start = ((), (), s32[]{:S(2)}) async-start(), calls=%async_computation.3 | async-start | bytes 1638400 | tf_op jit(solution)/shard_map/all_gather | solution.py:49
  10.1 5.4 %copy-start.6 = (s32[64,4]{0,1:T(4,128)S(1)}, s32[64,4]{0,1:T(4,128)}, u32[]{:S(2)}) copy-start(s32[64,4]{0,1:T(4,128)} %param.19) | copy-start | bytes 3076
  10.1 64.4 %all-to-all-start.1 = ((f32[4,10,128,128]{3,2,1,0:T(8,128)}), f32[4,10,128,128]{3,2,1,0:T(8,128)S(1)}, u32[]{:S(2)}, u32[]{:S(2)}) async-start(f32[4,10,128,128]{3,2,1,0:T(8,128)} %stack.2), calls=%async_computation.1 | async-start | bytes 5242880 | tf_op jit(solution)/shard_map/all_to_all | solution.py:51
  15.8 3.2 %copy-start.11 = (s32[64]{0:T(128)S(1)}, s32[64]{0:T(128)}, u32[]{:S(2)}) copy-start(s32[64]{0:T(128)} %param.18) | copy-start | bytes 772
  17.6 4.1 %copy-start.10 = (s32[64]{0:T(128)S(1)}, s32[64]{0:T(128)}, u32[]{:S(2)}) copy-start(s32[64]{0:T(128)} %param.17) | copy-start | bytes 772
  17.6 4.1 %copy-start.5 = (f32[10,64,64]{2,1,0:T(8,128)S(1)}, f32[10,64,64]{2,1,0:T(8,128)}, u32[]{:S(2)}) copy-start(f32[10,64,64]{2,1,0:T(8,128)} %param.22) | copy-start | bytes 491524
  71.0 3.4 %copy-start.9 = (s32[128]{0:T(128)S(1)}, s32[128]{0:T(128)}, u32[]{:S(2)}) copy-start(s32[128]{0:T(128)} %constant.168) | copy-start | bytes 1540
  71.1 3.4 %copy-start.8 = (s32[128]{0:T(128)S(1)}, s32[128]{0:T(128)}, u32[]{:S(2)}) copy-start(s32[128]{0:T(128)} %constant.169) | copy-start | bytes 1540
  71.1 3.4 %copy-start.7 = (s32[128]{0:T(128)S(1)}, s32[128]{0:T(128)}, u32[]{:S(2)}) copy-start(s32[128]{0:T(128)} %constant.170) | copy-start | bytes 1540
  74.6 82.8 %all-to-all-start = ((s32[128,1,3]{2,1,0:T(1,128)}), s32[128,1,3]{2,1,0:T(1,128)S(1)}, u32[]{:S(2)}, u32[]{:S(2)}) async-start(s32[128,1,3]{2,1,0:T(1,128)} %bitcast.4), calls=%async_computation | async-start | bytes 131072 | tf_op jit(solution)/shard_map/all_to_all | solution.py:98
  87.5 4.9 %copy-start.2 = (f32[64,128,128]{2,1,0:T(8,128)S(1)}, f32[64,128,128]{2,1,0:T(8,128)}, u32[]{:S(2)}) copy-start(f32[64,128,128]{2,1,0:T(8,128)} %gather_fusion.1) | copy-start | bytes 12582916
  87.6 4.9 %copy-start.3 = (f32[64,64,128]{2,1,0:T(8,128)S(1)}, f32[64,64,128]{2,1,0:T(8,128)}, u32[]{:S(2)}) copy-start(f32[64,64,128]{2,1,0:T(8,128)} %param.25) | copy-start | bytes 6291460
  123.6 3.7 %copy-start.4 = (f32[128,64,32]{1,2,0:T(8,128)S(1)}, f32[128,64,32]{1,2,0:T(8,128)}, u32[]{:S(2)}) copy-start(f32[128,64,32]{1,2,0:T(8,128)} %gather_fusion.5) | copy-start | bytes 3145732
  157.4 117.6 %all-to-all-start.2 = ((f32[128,3,4096]{2,1,0:T(4,128)}), f32[128,3,4096]{2,1,0:T(4,128)}, u32[]{:S(2)}, u32[]{:S(2)}) async-start(f32[128,3,4096]{2,1,0:T(4,128)} %copy.103), calls=%async_computation.2 | async-start | bytes 16777216 | tf_op jit(solution)/shard_map/all_to_all | solution.py:91
  301.6 5.3 %copy-start.1 = (s32[16384]{0:T(1024)S(1)}, s32[16384]{0:T(1024)}, u32[]{:S(2)}) copy-start(s32[16384]{0:T(1024)} %param.20) | copy-start | bytes 196612
Sparse Core Ops, SparseCore 0:
  9.0 51.6 all-gather.1
